TPU v7x, 32 devices: a whole 2x2x4 slice. The times are simulated.
32 devices in a mesh: groups: 2 (over x), shot: 16 (over z, y, core).
Axes of the slice: x: 2, y: 2, z: 4, core: 2. Of those that a mesh axis runs over, the one named last changes fastest.
Arguments:
- blended: bfloat16 [32, 768, 512], P(('groups', 'shot')), parts along dimension 0, may hold values from -6 to 6
- partners: int32 [32], P(('groups', 'shot')), parts along dimension 0, may hold values from 0 to 15, as said below
- delays: int32 [32], P(('groups', 'shot')), parts along dimension 0, may hold values from 0 to 255
- time_taps: float32 [16, 5], replicated, may hold values from -2.5 to 2.5
- time_bias: float32 [16], replicated, may hold values from -0.5 to 0.5
- shot_taps: float32 [16, 5], replicated, may hold values from -2.5 to 2.5
- mix_weight: float32 [16, 16], replicated, may hold values from -1.5 to 1.5
- mix_bias: float32 [16], replicated, may hold values from -0.5 to 0.5
- up_taps: float32 [16, 5], replicated, may hold values from -0.875 to 0.875
Outputs:
- deblended: bfloat16 [32, 768, 512], P(('groups', 'shot')), parts along dimension 0
There are 2 independent parts, one for each index of `groups`. A program takes and returns all parts, laid end to end along the dimension named above; an argument that names none is the same for every part. Nothing has to cross between parts.
Inputs may be any that keep to these rules, and one draw needn't show every extreme that they name: partners[s] is never s and lies at most 1 shots away from s in firing order; that distance is reached.
All inputs are finite; a program needn't handle non-finite values.
Results may differ from a plain program's by a relative error of at most 0.0053.
Values may be sent and summed in bfloat16 or wider, within the bound.
No kernel may reach another device: no remote copies, remote signals or barrier semaphores. Data moves between devices by JAX's collectives and lax.ppermute only.
A program may use at most 64 MiB of HBM per device.

v0:
```python
import jax
import jax.numpy as jnp
from jax import lax
from jax.sharding import PartitionSpec as P

ITERS = 2


def with_halo(shard, sides, width):
    for axis, dim in sides:
        size, length = (lax.axis_size(axis), shard.shape[dim])
        up = [(i, (i + 1) % size) for i in range(size - 1)]
        down = [(j, i) for i, j in up]
        last = lax.slice_in_dim(shard, length - width, length, axis=dim)
        initial = lax.slice_in_dim(shard, 0, width, axis=dim)
        before = lax.ppermute(last, axis, up)
        after = lax.ppermute(initial, axis, down)
        shard = jnp.concatenate([before, shard, after], axis=dim)
    return shard


def shifted_back(values):
    return jnp.pad(values[..., :-1], [(0, 0)] * (values.ndim - 1) + [(1, 0)])


def shifted_ahead(values):
    return jnp.pad(values[..., 1:], [(0, 0)] * (values.ndim - 1) + [(0, 1)])


def shot_neighbour(values, offset):
    if offset > 0:
        return jnp.pad(values[:, :, offset:, :], ((0, 0), (0, 0), (0, offset), (0, 0)))
    if offset < 0:
        return jnp.pad(values[:, :, :offset, :], ((0, 0), (0, 0), (-offset, 0), (0, 0)))
    return values


def denoise_images(images, time_taps, time_bias, shot_taps, mix_weight, mix_bias, up_taps):
    even_part = images[..., 0::2]
    odd_part = images[..., 1::2]
    planes = (
        shifted_back(even_part),
        shifted_back(odd_part),
        even_part,
        odd_part,
        shifted_ahead(even_part),
    )
    total = jnp.zeros(
        (images.shape[0], time_taps.shape[0], images.shape[1], even_part.shape[2]), jnp.float32
    )
    total = total + time_bias[None, :, None, None]
    for tap_index in range(5):
        total = total + time_taps[None, :, tap_index, None, None] * planes[tap_index][:, None]
    strided = jax.nn.relu(total)
    across = jnp.zeros_like(strided)
    for tap_index in range(5):
        across = across + shot_taps[None, :, tap_index, None, None] * shot_neighbour(
            strided, tap_index - 2
        )
    mixed_act = jnp.einsum("dc,gcsh->gdsh", mix_weight, across, precision=lax.Precision.HIGHEST)
    mixed_act = jax.nn.relu(mixed_act + mix_bias[None, :, None, None])
    projected = jnp.einsum("ck,gcsh->gksh", up_taps, mixed_act, precision=lax.Precision.HIGHEST)
    even_out = shifted_ahead(projected[:, 0]) + projected[:, 2] + shifted_back(projected[:, 4])
    odd_out = shifted_ahead(projected[:, 1]) + projected[:, 3]
    joined = jnp.stack([even_out, odd_out], axis=-1).reshape(images.shape)
    return images - joined


def delay_traces(traces, delays):
    lead = traces.shape[2] // 2
    padded = jnp.pad(traces, ((0, 0), (0, 0), (lead, 0)))

    def one_shot(trace_set, delay):
        return lax.dynamic_slice_in_dim(trace_set, lead - delay, traces.shape[2], axis=1)

    return jax.vmap(one_shot)(padded, delays)


def reblend(denoised, record, partner_rows, delays):
    delayed = delay_traces(partner_rows, delays).astype(jnp.float32)
    value = denoised.astype(jnp.float32)
    return (value + 0.5 * (record.astype(jnp.float32) - value - delayed)).astype(jnp.bfloat16)


def body(blended, partners, delays, time_taps, time_bias, shot_taps, mix_weight, mix_bias, up_taps):
    shot_count = blended.shape[0]
    first_shot = lax.axis_index("shot") * shot_count
    peers = lax.axis_size("shot")
    rcv_total = blended.shape[1]
    time_len = blended.shape[2]

    def one_receiver(image):
        cleaned = denoise_images(
            image[None].astype(jnp.float32),
            time_taps,
            time_bias,
            shot_taps,
            mix_weight,
            mix_bias,
            up_taps,
        )
        return cleaned[0].astype(jnp.bfloat16)

    def denoise_block(received):
        images = jnp.moveaxis(received, 1, 0)
        cleaned = lax.map(one_receiver, images)
        return jnp.moveaxis(cleaned, 0, 1)

    current = blended
    local_index = partners - first_shot + shot_count
    for iteration in range(ITERS):
        arranged = current.reshape(shot_count, peers, rcv_total // peers, time_len)
        denoise_cleaned = denoise_block(
            lax.all_to_all(arranged, "shot", split_axis=1, concat_axis=0, tiled=True)[:, 0]
        )
        in_pieces = denoise_cleaned[:, None]
        in_gathers = in_pieces[:, 0]
        denoised = lax.all_to_all(in_gathers, "shot", split_axis=0, concat_axis=1, tiled=True)
        nearby = with_halo(denoised, (("shot", 0),), shot_count)
        partner_rows = jnp.take(nearby, local_index, axis=0)
        current = reblend(denoised, blended, partner_rows, delays)
    return current


def solution(mesh):
    placed = (
        P(("groups", "shot"), None, None),
        P(("groups", "shot")),
        P(("groups", "shot")),
        P(),
        P(),
        P(),
        P(),
        P(),
        P(),
    )
    return jax.shard_map(
        body,
        mesh=mesh,
        in_specs=placed,
        out_specs=P(("groups", "shot"), None, None),
        check_vma=False,
    )
```

profile of v0, /device:TPU:1, one launch (start us, length us, event | category | flops | bytes accessed | tf_op | source)
XLA Modules:
  0.0 431.5 jit_solution(12231934488587156489)
XLA Ops:
  0.0 7.3 %all-to-all-start = ((bf16[1,16,48,512]{3,2,0,1:T(8,128)(2,1)}), bf16[1,16,48,512]{3,2,0,1:T(8,128)(2,1)S(1)}, u32[]{:S(2)}, u32[]{:S(2)}) async-start(bf16[1,16,48,512]{3,2,0,1:T(8,128)(2,1)} %bitcast.290), calls=%async_computation | async-start | bytes 1572864 | tf_op jit(solution)/shard_map/all_to_all | solution.py:114
  7.4 18.5 %all-to-all-done = bf16[1,16,48,512]{3,2,0,1:T(8,128)(2,1)S(1)} async-done(((bf16[1,16,48,512]{3,2,0,1:T(8,128)(2,1)}), bf16[1,16,48,512]{3,2,0,1:T(8,128)(2,1)S(1)}, u32[]{:S(2)}, u32[]{:S(2)}) %all-to-all-start) | async-done | bytes 786464 | tf_op jit(solution)/shard_map/all_to_all | solution.py:114
  26.0 143.1 %while.27 = (s32[]{:T(128)}, bf16[48,16,512]{2,0,1:T(8,128)(2,1)S(1)}, bf16[48,16,512]{2,0,1:T(8,128)(2,1)S(1)}, f32[16,5]{0,1:T(8,128)S(1)}, f32[16]{0:T(128)S(...) while((s32[]{:T(128)}, ...), condition=%wide.region_1.2_spmd, body=%wide.region_0.1_spmd.sunk | while | flops 18722816 | bytes 4885429 | solution.py:106
  27.2 0.6 fusion.105
  30.2 0.6 fusion.105
  33.2 0.6 fusion.105
  169.1 26.1 %all_to_all.42 = bf16[16,48,512]{2,1,0:T(8,128)(2,1)S(1)} all-to-all(bf16[16,48,512]{2,1,0:T(8,128)(2,1)S(1)} %bitcast.292), channel_id=1, replica_groups=mesh['groups'=2,'shot'=16] {'shot'}, dimensions={0} | all-to-all | bytes 1572864 | tf_op jit(solution)/shard_map/all_to_all | solution.py:118
  195.2 2.2 collective-permute-start
  197.4 2.2 collective-permute-start.1
  200.9 13.8 %collective-permute-done = bf16[1,768,512]{2,1,0:T(8,128)(2,1)S(1)} collective-permute-done((bf16[1,768,512]{2,1,0:T(8,128)(2,1)S(1)}, bf16[1,768,512]{2,1,0:T(8,128)(2,1)S(1)}, u32[]{:S(2)}, u32[]{:S(2)}) %collective-permute-start) | collective-permute-done | bytes 786464 | tf_op jit(solution)/shard_map/ppermute | solution.py:16
  215.2 0.7 copy-done
  215.8 1.6 fusion.60
  217.4 5.6 %all-to-all-start.2 = ((bf16[1,16,48,512]{3,2,0,1:T(8,128)(2,1)}), bf16[1,16,48,512]{3,2,0,1:T(8,128)(2,1)S(1)}, u32[]{:S(2)}, u32[]{:S(2)}) async-start(bf16[1,16,48,512]{3,2,0,1:T(8,128)(2,1)} %bitcast.74), calls=%async_computation.2 | async-start | bytes 1572864 | tf_op jit(solution)/shard_map/all_to_all | solution.py:114
  223.1 18.6 %all-to-all-done.2 = bf16[1,16,48,512]{3,2,0,1:T(8,128)(2,1)S(1)} async-done(((bf16[1,16,48,512]{3,2,0,1:T(8,128)(2,1)}), bf16[1,16,48,512]{3,2,0,1:T(8,128)(2,1)S(1)}, u32[]{:S(2)}, u32[]{:S(2)}) %all-to-all-start.2) | async-done | bytes 786464 | tf_op jit(solution)/shard_map/all_to_all | solution.py:114
  241.7 142.1 %while.28 = (s32[]{:T(128)}, bf16[48,16,512]{2,0,1:T(8,128)(2,1)S(1)}, bf16[48,16,512]{2,0,1:T(8,128)(2,1)S(1)}, f32[16,5]{0,1:T(8,128)S(1)}, f32[16]{0:T(128)S(...) while((s32[]{:T(128)}, ...), condition=%wide.region_3.5_spmd, body=%wide.region_2.4_spmd.sunk | while | flops 18722816 | bytes 4885429 | solution.py:106
  251.7 0.6 fusion.114
  263.6 0.6 fusion.114
  275.4 0.6 fusion.114
  287.3 0.6 fusion.114
  299.1 0.6 fusion.114
  310.9 0.6 fusion.114
  322.8 0.6 fusion.114
  334.6 0.6 fusion.114
  346.5 0.6 fusion.114
  358.3 0.6 fusion.114
  370.1 0.6 fusion.114
  382.0 0.6 fusion.114
  383.8 26.1 %all_to_all.43 = bf16[16,48,512]{2,1,0:T(8,128)(2,1)S(1)} all-to-all(bf16[16,48,512]{2,1,0:T(8,128)(2,1)S(1)} %bitcast.291), channel_id=1, replica_groups=mesh['groups'=2,'shot'=16] {'shot'}, dimensions={0} | all-to-all | bytes 1572864 | tf_op jit(solution)/shard_map/all_to_all | solution.py:118
  409.9 2.2 collective-permute-start.2
  412.0 2.2 collective-permute-start.3
  414.2 15.1 %collective-permute-done.2 = bf16[1,768,512]{2,1,0:T(8,128)(2,1)S(1)} collective-permute-done((bf16[1,768,512]{2,1,0:T(8,128)(2,1)S(1)}, bf16[1,768,512]{2,1,0:T(8,128)(2,1)S(1)}, u32[]{:S(2)}, u32[]{:S(2)}) %collective-permute-start.2) | collective-permute-done | bytes 786464 | tf_op jit(solution)/shard_map/ppermute | solution.py:16
  429.8 1.6 fusion.65
  (2596 shorter events, 260.6 us)
Async XLA Ops:
  0.0 25.9 %all-to-all-start = ((bf16[1,16,48,512]{3,2,0,1:T(8,128)(2,1)}), bf16[1,16,48,512]{3,2,0,1:T(8,128)(2,1)S(1)}, u32[]{:S(2)}, u32[]{:S(2)}) async-start(bf16[1,16,48,512]{3,2,0,1:T(8,128)(2,1)} %bitcast.290), calls=%async_computation | async-start | bytes 1572864 | tf_op jit(solution)/shard_map/all_to_all | solution.py:114
  7.3 18.6 %copy-start.1 = (f32[16,5]{0,1:T(8,128)S(1)}, f32[16,5]{0,1:T(8,128)}, u32[]{:S(2)}) copy-start(f32[16,5]{0,1:T(8,128)} %param.23) | copy-start | bytes 964
  7.4 18.6 %copy-start.2 = (f32[16,5]{0,1:T(8,128)S(1)}, f32[16,5]{0,1:T(8,128)}, u32[]{:S(2)}) copy-start(f32[16,5]{0,1:T(8,128)} %param.20) | copy-start | bytes 964
  7.4 18.6 %copy-start.3 = (f32[16,5]{0,1:T(8,128)S(1)}, f32[16,5]{0,1:T(8,128)}, u32[]{:S(2)}) copy-start(f32[16,5]{0,1:T(8,128)} %param.18) | copy-start | bytes 964
  7.4 18.6 %copy-start.4 = (f32[16]{0:T(128)S(1)}, f32[16]{0:T(128)}, u32[]{:S(2)}) copy-start(f32[16]{0:T(128)} %param.19) | copy-start | bytes 196
  7.4 18.6 %copy-start.5 = (f32[16,16]{1,0:T(8,128)S(1)}, f32[16,16]{1,0:T(8,128)}, u32[]{:S(2)}) copy-start(f32[16,16]{1,0:T(8,128)} %param.21) | copy-start | bytes 3076
  7.4 18.6 %copy-start.6 = (f32[16]{0:T(128)S(1)}, f32[16]{0:T(128)}, u32[]{:S(2)}) copy-start(f32[16]{0:T(128)} %param.22) | copy-start | bytes 196
  195.2 19.5 %collective-permute-start = (bf16[1,768,512]{2,1,0:T(8,128)(2,1)S(1)}, bf16[1,768,512]{2,1,0:T(8,128)(2,1)S(1)}, u32[]{:S(2)}, u32[]{:S(2)}) collective-permute-start(bf16[1,768,512]{2,1,0:T(8,128)(2,1)S(1)} %bitcast.282), channel_id=1, source_target_pairs={{0,1},{1,2},{2,3},{3,4},{4,5},{5,6},{6,7},{7,8},{8,9},{9,10},{10,1... | collective-permute-start | bytes 2359304 | tf_op jit(solution)/shard_map/ppermute | solution.py:16
  197.4 17.3 %collective-permute-start.1 = (bf16[1,768,512]{2,1,0:T(8,128)(2,1)S(1)}, bf16[1,768,512]{2,1,0:T(8,128)(2,1)S(1)}, u32[]{:S(2)}, u32[]{:S(2)}) collective-permute-start(bf16[1,768,512]{2,1,0:T(8,128)(2,1)S(1)} %bitcast.283), channel_id=1, source_target_pairs={{1,0},{2,1},{3,2},{4,3},{5,4},{6,5},{7,6},{8,7},{9,8},{10,9},{11,1... | collective-permute-start | bytes 2359304 | tf_op jit(solution)/shard_map/ppermute | solution.py:17
  214.7 1.1 copy-start
  217.4 24.2 %all-to-all-start.2 = ((bf16[1,16,48,512]{3,2,0,1:T(8,128)(2,1)}), bf16[1,16,48,512]{3,2,0,1:T(8,128)(2,1)S(1)}, u32[]{:S(2)}, u32[]{:S(2)}) async-start(bf16[1,16,48,512]{3,2,0,1:T(8,128)(2,1)} %bitcast.74), calls=%async_computation.2 | async-start | bytes 1572864 | tf_op jit(solution)/shard_map/all_to_all | solution.py:114
  409.9 19.5 %collective-permute-start.2 = (bf16[1,768,512]{2,1,0:T(8,128)(2,1)S(1)}, bf16[1,768,512]{2,1,0:T(8,128)(2,1)S(1)}, u32[]{:S(2)}, u32[]{:S(2)}) collective-permute-start(bf16[1,768,512]{2,1,0:T(8,128)(2,1)S(1)} %bitcast.286), channel_id=1, source_target_pairs={{0,1},{1,2},{2,3},{3,4},{4,5},{5,6},{6,7},{7,8},{8,9},{9,10},{10,1... | collective-permute-start | bytes 2359304 | tf_op jit(solution)/shard_map/ppermute | solution.py:16
  412.0 17.3 %collective-permute-start.3 = (bf16[1,768,512]{2,1,0:T(8,128)(2,1)S(1)}, bf16[1,768,512]{2,1,0:T(8,128)(2,1)S(1)}, u32[]{:S(2)}, u32[]{:S(2)}) collective-permute-start(bf16[1,768,512]{2,1,0:T(8,128)(2,1)S(1)} %bitcast.287), channel_id=1, source_target_pairs={{1,0},{2,1},{3,2},{4,3},{5,4},{6,5},{7,6},{8,7},{9,8},{10,9},{11,1... | collective-permute-start | bytes 2359304 | tf_op jit(solution)/shard_map/ppermute | solution.py:17
where the time goes:
time: 433 us; the launch traced here: 431 us
  local copies, waits for them, and re-layouts  151 us (35%)
  matrix products  85.4 us (20%)
  waiting for transfers between devices  66 us (15%)
  blocking collectives  52.1 us (12%)
  other arithmetic  37.6 us (9%)
  starting transfers between devices  21.7 us (5%)
  loops' own time  16.5 us (4%)
    dot_general x96, matrix products, denoise_images(): jnp.einsum('dc,gcsh->gdsh', mix_weight, across, precision=lax.Precision.H...  58.8 us
    all_to_all x2, blocking collectives, body(): lax.all_to_all(in_gathers, 'shot', split_axis=0, concat_axis=1, tiled=True)  52.1 us
    all_to_all x2, waiting for transfers between devices, body(): lax.all_to_all(arranged, 'shot', split_axis=1, concat_axis=0, tiled=True)  37 us
    mul x768, local copies, waits for them, and re-layouts, denoise_images(): time_taps[None, :, tap_index, None, None] * planes[tap_index][:, None]  36.6 us
    ppermute x2, waiting for transfers between devices, with_halo(): before = lax.ppermute(last, axis, up)  28.9 us
    dynamic_update_slice x192, local copies, waits for them, and re-layouts, denoise_block(): cleaned = lax.map(one_receiver, images)  28.9 us
    dot_general x96, matrix products, denoise_images(): jnp.einsum('ck,gcsh->gksh', up_taps, mixed_act, precision=lax.Precision.H...  26.6 us
    slice x192, local copies, waits for them, and re-layouts, shifted_ahead(): return jnp.pad(values[..., 1:], [(0, 0)] * (values.ndim - 1) + [(0, 1)])  17.8 us
  transfers between devices with their start and end apart: 6, of which 4 were waited for; matrix products, arithmetic and copies ran while one was open for 0% of the time, Pallas kernels for 0%

commit v1 on v0

v1 whole, which is shorter than its diff:
```python
import jax
import jax.numpy as jnp
from jax import lax
from jax.experimental import pallas as pl
from jax.experimental.pallas import tpu as pltpu
from jax.sharding import PartitionSpec as P

ITERS = 2
LANES = 128
UB = 8
HALVES = 2
TILES = 4
ONES_LANE = (96, 32)


def split_pair(value):
    high = value.astype(jnp.bfloat16)
    low = (value - high.astype(jnp.float32)).astype(jnp.bfloat16)
    return high, low


def prepare_kernel(lane_ref, mix_ref, up_ref, first_ref, mixing_ref, last_ref):
    for half in range(HALVES):
        row = lax.broadcasted_iota(jnp.int32, (LANES, TILES * LANES), 0)
        col = lax.broadcasted_iota(jnp.int32, (LANES, TILES * LANES), 1)
        sample = half * 32 + (col // LANES) * UB + col % UB
        taps = jnp.concatenate([lane_ref[...]] * TILES, axis=1)
        total = jnp.where(row == ONES_LANE[half], taps[5:6], 0.0)
        for k in range(5):
            total = total + jnp.where(row == ((2 * sample + k - 2) & (LANES - 1)), taps[k : k + 1], 0.0)
        high, low = split_pair(total)
        first_ref[half, :LANES, :] = high
        first_ref[half, LANES:, :] = low

        row = lax.broadcasted_iota(jnp.int32, (TILES * LANES, LANES), 0)
        col = lax.broadcasted_iota(jnp.int32, (TILES * LANES, LANES), 1)
        sample = half * 32 + (row // LANES) * UB + row % UB
        taps = jnp.concatenate([up_ref[...]] * TILES, axis=0)
        total = jnp.zeros((TILES * LANES, LANES), jnp.float32)
        for k in range(5):
            total = total + jnp.where(col == ((2 * sample + k - 2) & (LANES - 1)), taps[:, k : k + 1], 0.0)
        high, low = split_pair(total)
        last_ref[half, :, :LANES] = high
        last_ref[half, :, LANES:] = low

    row = lax.broadcasted_iota(jnp.int32, (LANES, LANES), 0)
    col = lax.broadcasted_iota(jnp.int32, (LANES, LANES), 1)
    high, low = split_pair(jnp.where(row % UB == col % UB, mix_ref[...], 0.0))
    mixing_ref[:LANES, :LANES] = high
    mixing_ref[LANES:, :LANES] = high
    mixing_ref[:LANES, LANES:] = low
    mixing_ref[LANES:, LANES:] = low


def prepare(time_taps, time_bias, shot_taps, mix_weight, mix_bias, up_taps):
    lanes = jnp.concatenate(
        [time_taps.T, time_bias[None], shot_taps.T, mix_bias[None], jnp.zeros((4, time_bias.shape[0]), jnp.float32)]
    )
    lanes = jnp.repeat(lanes, UB, axis=1)
    mix = jnp.repeat(jnp.repeat(mix_weight.T, UB, axis=0), UB, axis=1)
    up = jnp.repeat(up_taps, UB, axis=0)
    mats = pl.pallas_call(
        prepare_kernel,
        out_shape=(
            jax.ShapeDtypeStruct((HALVES, 2 * LANES, TILES * LANES), jnp.bfloat16),
            jax.ShapeDtypeStruct((2 * LANES, 2 * LANES), jnp.bfloat16),
            jax.ShapeDtypeStruct((HALVES, TILES * LANES, 2 * LANES), jnp.bfloat16),
        ),
        cost_estimate=pl.CostEstimate(flops=4_000_000, bytes_accessed=2_000_000, transcendentals=0),
    )(lanes, mix, up)
    return (lanes,) + mats


def deblend_kernel(
    shots, rcv, blocks,
    partner_ref, delay_ref, record_ref, lane_ref, first_ref, mixing_ref, last_ref, out_ref,
    current, strided, mixed_high, mixed_low, correction, denoised,
):
    rows = shots * rcv
    time_len = blocks * LANES
    halo = 2 * rcv
    zero_block = jnp.zeros((rows, LANES), jnp.bfloat16)
    current[:, :LANES] = zero_block
    current[:, (blocks + 1) * LANES :] = zero_block
    current[:, LANES : (blocks + 1) * LANES] = record_ref[...]
    strided[:halo, :] = jnp.zeros((halo, HALVES * TILES * LANES), jnp.float32)
    strided[halo + rows :, :] = jnp.zeros((halo, HALVES * TILES * LANES), jnp.float32)
    for half in range(HALVES):
        correction[half, :, :LANES] = jnp.zeros((rows, LANES), jnp.float32)
        correction[half, :, (blocks + 1) * LANES :] = jnp.zeros((rows, LANES), jnp.float32)
    lane = lax.broadcasted_iota(jnp.int32, (rows, LANES), 1)

    def one_block(block, carry):
        at = pl.multiple_of(block * LANES, LANES)
        before = current[:, pl.ds(at, LANES)]
        here = current[:, pl.ds(pl.multiple_of(at + LANES, LANES), LANES)]
        after = current[:, pl.ds(pl.multiple_of(at + 2 * LANES, LANES), LANES)]
        one = jnp.ones_like(here)
        windows = (
            jnp.where(lane >= LANES - 2, before, jnp.where(lane == ONES_LANE[0], one, here)),
            jnp.where(lane == 0, after, jnp.where(lane == ONES_LANE[1], one, here)),
        )
        for half in range(HALVES):
            window = jnp.concatenate([windows[half]] * 2, axis=1)
            total = jnp.dot(window, first_ref[half], preferred_element_type=jnp.float32)
            strided[halo : halo + rows, half * TILES * LANES : (half + 1) * TILES * LANES] = jnp.maximum(total, 0.0)

        def one_tile(tile, carry):
            at = pl.multiple_of(tile * LANES, LANES)
            across = None
            for k in range(5):
                term = strided[k * rcv : k * rcv + rows, pl.ds(at, LANES)] * lane_ref[6 + k : 7 + k, :]
                across = term if across is None else across + term
            high, low = split_pair(across)
            both = jnp.dot(jnp.concatenate([high, low], axis=1), mixing_ref[...], preferred_element_type=jnp.float32)
            mixed = jnp.maximum(both[:, :LANES] + both[:, LANES:] + lane_ref[11:12, :], 0.0)
            high, low = split_pair(mixed)
            mixed_high[:, pl.ds(at, LANES)] = high
            mixed_low[:, pl.ds(at, LANES)] = low
            return carry

        lax.fori_loop(0, HALVES * TILES, one_tile, 0)
        at = pl.multiple_of((block + 1) * LANES, LANES)
        for half in range(HALVES):
            span = slice(half * TILES * LANES, (half + 1) * TILES * LANES)
            both = jnp.dot(mixed_high[:, span], last_ref[half], preferred_element_type=jnp.float32)
            both = both + jnp.dot(mixed_low[:, span], last_ref[half], preferred_element_type=jnp.float32)
            correction[half, :, pl.ds(at, LANES)] = both[:, :LANES] + both[:, LANES:]
        return carry

    def one_iteration(iteration, carry):
        lax.fori_loop(0, blocks, one_block, 0)
        for block in range(blocks):
            at = (block + 1) * LANES
            low_half = jnp.where(lane < 96, correction[0, :, at : at + LANES], correction[0, :, at + LANES : at + 2 * LANES])
            high_half = jnp.where(lane >= 32, correction[1, :, at : at + LANES], correction[1, :, at - LANES : at])
            value = current[:, at : at + LANES].astype(jnp.float32) - (low_half + high_half)
            denoised[:, at - LANES : at] = value.astype(jnp.bfloat16)
        column = lax.broadcasted_iota(jnp.int32, (rcv, time_len), 1)

        def one_shot(shot, carry):
            delay = delay_ref[shot]
            here = pl.ds(pl.multiple_of(shot * rcv, rcv), rcv)
            there = pl.ds(pl.multiple_of(partner_ref[shot] * rcv, rcv), rcv)
            shifted = pltpu.roll(denoised[there, :].astype(jnp.float32), delay, 1)
            delayed = jnp.where(column >= delay, shifted, 0.0)
            value = denoised[here, :].astype(jnp.float32)
            record = record_ref[here, :].astype(jnp.float32)
            current[here, LANES : LANES + time_len] = (value + 0.5 * (record - value - delayed)).astype(jnp.bfloat16)
            return carry

        lax.fori_loop(0, shots, one_shot, 0)
        return carry

    lax.fori_loop(0, ITERS, one_iteration, 0)
    out_ref[...] = current[:, LANES : LANES + time_len]


def deblend(record, partners, delays, lanes, first, mixing, last, shots, rcv):
    rows, time_len = record.shape
    blocks = time_len // LANES
    wide = HALVES * TILES * LANES
    vmem = pl.BlockSpec(memory_space=pltpu.VMEM)
    smem = pl.BlockSpec(memory_space=pltpu.SMEM)

    def kernel(*refs):
        deblend_kernel(shots, rcv, blocks, *refs)

    return pl.pallas_call(
        kernel,
        out_shape=jax.ShapeDtypeStruct((rows, time_len), jnp.bfloat16),
        in_specs=[smem, smem, vmem, vmem, vmem, vmem, vmem],
        out_specs=vmem,
        scratch_shapes=[
            pltpu.VMEM((rows, (blocks + 2) * LANES), jnp.bfloat16),
            pltpu.VMEM((rows + 4 * rcv, wide), jnp.float32),
            pltpu.VMEM((rows, wide), jnp.bfloat16),
            pltpu.VMEM((rows, wide), jnp.bfloat16),
            pltpu.VMEM((HALVES, rows, (blocks + 2) * LANES), jnp.float32),
            pltpu.VMEM((rows, time_len), jnp.bfloat16),
        ],
        compiler_params=pltpu.CompilerParams(vmem_limit_bytes=48 << 20),
        cost_estimate=pl.CostEstimate(
            flops=ITERS * rows * time_len * 8 * 2 * 256 * 5, bytes_accessed=4 * rows * time_len, transcendentals=0
        ),
    )(partners, delays, record, lanes, first, mixing, last)


def body(blended, partners, delays, time_taps, time_bias, shot_taps, mix_weight, mix_bias, up_taps):
    shot_count, rcv_total, time_len = blended.shape
    peers = lax.axis_size("shot")
    shots = shot_count * peers
    rcv = rcv_total // peers
    padded = -(-rcv // 16) * 16
    orders = lax.all_gather(jnp.stack([partners, delays]), "shot", axis=1, tiled=True)
    mats = prepare(time_taps, time_bias, shot_taps, mix_weight, mix_bias, up_taps)
    pieces = jnp.moveaxis(blended.reshape(shot_count, peers, rcv, time_len), 1, 0)
    gathers = lax.all_to_all(pieces, "shot", split_axis=0, concat_axis=0, tiled=True).reshape(shots, rcv, time_len)
    gathers = jnp.pad(gathers, ((0, 0), (0, padded - rcv), (0, 0)))
    done = deblend(gathers.reshape(shots * padded, time_len), orders[0], orders[1], *mats, shots, padded)
    done = done.reshape(shots, padded, time_len)[:, :rcv]
    pieces = done.reshape(peers, shot_count, rcv, time_len)
    back = lax.all_to_all(pieces, "shot", split_axis=0, concat_axis=0, tiled=True)
    return jnp.moveaxis(back, 0, 1).reshape(shot_count, rcv_total, time_len)


def solution(mesh):
    placed = (
        P(("groups", "shot"), None, None),
        P(("groups", "shot")),
        P(("groups", "shot")),
        P(),
        P(),
        P(),
        P(),
        P(),
        P(),
    )
    return jax.shard_map(
        body,
        mesh=mesh,
        in_specs=placed,
        out_specs=P(("groups", "shot"), None, None),
        check_vma=False,
    )
```

time: 433 us -> 111 us (0.26)
  local copies, waits for them, and re-layouts: 151 us -> 8.37 us
  matrix products: 85.4 us -> 0 us
  waiting for transfers between devices: 66 us -> 0.01 us
  Pallas kernels: 0 us -> 41.6 us
  other arithmetic: 37.6 us -> 0.07 us
  loops' own time: 16.5 us -> 0 us
  starting transfers between devices: 21.7 us -> 7.48 us
    dot_general x192 -> x0, matrix products: 85.4 us -> none  [the longest x96 58.8 us: denoise_images(): jnp.einsum('dc,gcsh->gdsh', mix_weight, across, precision=lax.Precision.H...]
    slice x672 -> x0, local copies, waits for them, and re-layouts: 48.8 us -> none  [the longest x192 17.8 us: shifted_ahead(): return jnp.pad(values[..., 1:], [(0, 0)] * (values.ndim - 1) + [(0, 1)])]
    pallas_call x0 -> x2, Pallas kernels: none -> 41.6 us  [the longest x1 38.5 us: deblend(): pl.pallas_call(kernel, out_shape=jax.ShapeDtypeStruct((rows, time_len), j...]
    all_to_all x2 -> x1, waiting for transfers between devices: 37 us -> 0.01 us  [body(): lax.all_to_all(pieces, 'shot', split_axis=0, concat_axis=0, tiled=True)]
    mul x768 -> x0, local copies, waits for them, and re-layouts: 36.6 us -> none  [denoise_images(): time_taps[None, :, tap_index, None, None] * planes[tap_index][:, None]]
    ppermute x4 -> x0, waiting for transfers between devices: 28.9 us -> none  [the longest x2 28.9 us: with_halo(): before = lax.ppermute(last, axis, up)]
    dynamic_update_slice x192 -> x0, local copies, waits for them, and re-layouts: 28.9 us -> none  [denoise_block(): cleaned = lax.map(one_receiver, images)]
    all_to_all x2 -> x1, blocking collectives: 52.1 us -> 25.1 us  [body(): lax.all_to_all(pieces, 'shot', split_axis=0, concat_axis=0, tiled=True)]
  transfers between devices with their start and end apart: 6 -> 1, of which waited for: 4 -> 0; matrix products, arithmetic and copies ran while one was open for 0% -> 2% of each run, Pallas kernels for 0% -> 3%
where the time goes in v1:
time: 111 us
  blocking collectives  51.8 us (47%)
  Pallas kernels  41.6 us (37%)
  local copies, waits for them, and re-layouts  8.37 us (8%)
  starting transfers between devices  7.48 us (7%)
  between operations  1.38 us (1%)
    pallas_call x1, Pallas kernels, deblend(): pl.pallas_call(kernel, out_shape=jax.ShapeDtypeStruct((rows, time_len), j...  38.5 us
    all_gather x1, blocking collectives, body(): lax.all_gather(jnp.stack([partners, delays]), 'shot', axis=1, tiled=True)  26.7 us
    all_to_all x1, blocking collectives, body(): lax.all_to_all(pieces, 'shot', split_axis=0, concat_axis=0, tiled=True)  25.1 us
    all_to_all x1, starting transfers between devices, body(): lax.all_to_all(pieces, 'shot', split_axis=0, concat_axis=0, tiled=True)  7.48 us
    unnamed x22, local copies, waits for them, and re-layouts  5.92 us
    pallas_call x1, Pallas kernels, prepare(): pl.pallas_call(prepare_kernel, out_shape=(jax.ShapeDtypeStruct((HALVES, 2...  3.08 us
  transfers between devices with their start and end apart: 1, of which 0 were waited for; matrix products, arithmetic and copies ran while one was open for 2% of the time, Pallas kernels for 3%

profile of v1, /device:TPU:1, one launch (start us, length us, event | category | flops | bytes accessed | tf_op | source)
XLA Modules:
  0.0 110.7 jit_solution(14933249099562523962)
XLA Ops:
  0.0 0.0 copy-start.8
  0.0 0.0 copy-start.9
  0.0 7.5 %all-to-all-start = ((bf16[16,1,48,512]{3,2,1,0:T(8,128)(2,1)}), bf16[16,1,48,512]{3,2,1,0:T(8,128)(2,1)S(1)}, u32[]{:S(2)}, u32[]{:S(2)}) async-start(bf16[16,1,48,512]{3,2,1,0:T(8,128)(2,1)} %bitcast.35), calls=%async_computation | async-start | bytes 1572864 | tf_op jit(solution)/shard_map/all_to_all | solution.py:198
  8.8 0.0 copy-start.5
  8.8 0.0 copy-start.6
  8.8 0.0 copy-done.8
  8.8 0.0 copy-done.9
  8.8 0.6 copy-done.5
  9.5 0.0 copy-done.6
  9.5 0.1 concatenate.3
  9.6 0.1 copy.28
  9.7 0.1 add_bitcast_fusion
  9.7 0.0 copy-start.4
  9.7 26.7 %all-gather = s32[16,1,2]{2,1,0:T(1,128)S(1)} all-gather(s32[1,1,2]{2,1,0:T(1,128)S(1)} %add_bitcast_fusion), channel_id=1, replica_groups=mesh['groups'=2,'shot'=16] {'shot'}, dimensions={0}, use_global_device_ids=true | all-gather | bytes 136 | tf_op jit(solution)/shard_map/all_gather | solution.py:195
  36.4 0.1 copy.27
  36.5 0.0 copy-done.4
  36.5 0.1 copy.29
  36.6 0.6 copy-done.7
  37.2 0.1 copy.31
  37.3 0.1 copy.30
  37.3 0.7 copy.33.mix_ref
  38.1 0.7 copy.34.lane_ref.refs_3_
  38.8 0.6 broadcast_bitcast_fusion.up_ref
  39.4 3.1 %shard_map.91 = (bf16[2,256,512]{2,1,0:T(8,128)(2,1)}, bf16[256,256]{1,0:T(8,128)(2,1)}, bf16[2,512,256]{2,1,0:T(8,128)(2,1)}) custom-call(f32[16,128]{1,0:T(8,128)} %copy.34.lane_ref.refs_3_, f32[128,128]{1,0:T(8,128)} %copy.33.mix_ref, f32[128,5]{1,0:T(8,128)} %broadcast_bitcast_fusion.up_ref), custom_call_target="tpu_custom_call" | custom-call | flops 4000000 | bytes 2000000 | tf_op jit(solution)/shard_map/pallas_call | solution.py:62
  42.5 0.0 all-to-all-done
  42.5 0.7 copy-done
  43.2 1.0 copy-done.1
  44.2 1.0 copy-done.2
  45.3 0.9 copy-done.3
  46.2 38.5 %shard_map.92 = bf16[768,512]{1,0:T(8,128)(2,1)S(1)} custom-call(s32[16]{0:T(128)S(1)} %get-tuple-element.12.refs_0_, s32[16]{0:T(128)S(1)} %get-tuple-element.11.refs_1_, bf16[768,512]{1,0:T(8,128)(2,1)S(1)} %bitcast.32, f32[16,128]{1,0:T(8,128)S(1)} %copy-done, bf16[2,256,512]{2,1,0:T(8,128)(2,1)S(1)} %copy-done.1, bf16[256,256]{1,0:T(8,128)(2,1)S(1)} %copy-done.3, ...), custom_call_target="tpu_custom_call" | custom-call | flops 16106127360 | bytes 1572864 | tf_op jit(solution)/shard_map/pallas_call | solution.py:169
  84.7 25.1 %all_to_all.10 = bf16[16,1,48,512]{3,2,1,0:T(8,128)(2,1)S(1)} all-to-all(bf16[16,1,48,512]{3,2,1,0:T(8,128)(2,1)S(1)} %bitcast.33), channel_id=1, replica_groups=mesh['groups'=2,'shot'=16] {'shot'}, dimensions={0} | all-to-all | bytes 1572864 | tf_op jit(solution)/shard_map/all_to_all | solution.py:203
  109.8 0.9 copy.39
  (10 shorter events, 0.0 us)
Async XLA Ops:
  0.0 8.8 %copy-start.8 = (f32[16]{0:T(128)S(1)}, f32[16]{0:T(128)}, u32[]{:S(2)}) copy-start(f32[16]{0:T(128)} %param.13) | copy-start | bytes 196
  0.0 8.8 %copy-start.9 = (f32[16]{0:T(128)S(1)}, f32[16]{0:T(128)}, u32[]{:S(2)}) copy-start(f32[16]{0:T(128)} %param.16) | copy-start | bytes 196
  0.0 42.5 %all-to-all-start = ((bf16[16,1,48,512]{3,2,1,0:T(8,128)(2,1)}), bf16[16,1,48,512]{3,2,1,0:T(8,128)(2,1)S(1)}, u32[]{:S(2)}, u32[]{:S(2)}) async-start(bf16[16,1,48,512]{3,2,1,0:T(8,128)(2,1)} %bitcast.35), calls=%async_computation | async-start | bytes 1572864 | tf_op jit(solution)/shard_map/all_to_all | solution.py:198
  8.8 0.7 copy-start.5
  8.8 0.7 copy-start.6
  9.7 26.8 %copy-start.4 = (f32[16,16]{1,0:T(8,128)S(1)}, f32[16,16]{1,0:T(8,128)}, u32[]{:S(2)}) copy-start(f32[16,16]{1,0:T(8,128)} %param.15) | copy-start | bytes 3076
  36.5 0.7 copy-start.7
  42.5 0.7 copy-start
  43.2 1.0 copy-start.1
  44.2 1.0 copy-start.2
  45.3 0.9 copy-start.3

commit v2 on v1

v2 whole, which is shorter than its diff:
```python
import jax
import jax.numpy as jnp
from jax import lax
from jax.experimental import pallas as pl
from jax.experimental.pallas import tpu as pltpu
from jax.sharding import PartitionSpec as P

ITERS = 2
LANES = 128
UB = 8
HALVES = 2
TILES = 4
ONES_LANE = (96, 32)


def split_pair(value):
    high = value.astype(jnp.bfloat16)
    low = (value - high.astype(jnp.float32)).astype(jnp.bfloat16)
    return high, low


def prepare_kernel(lane_ref, mix_ref, up_ref, first_ref, mixing_ref, last_ref):
    for half in range(HALVES):
        row = lax.broadcasted_iota(jnp.int32, (LANES, TILES * LANES), 0)
        col = lax.broadcasted_iota(jnp.int32, (LANES, TILES * LANES), 1)
        sample = half * 32 + (col // LANES) * UB + col % UB
        taps = jnp.concatenate([lane_ref[...]] * TILES, axis=1)
        total = jnp.where(row == ONES_LANE[half], taps[5:6], 0.0)
        for k in range(5):
            total = total + jnp.where(row == ((2 * sample + k - 2) & (LANES - 1)), taps[k : k + 1], 0.0)
        high, low = split_pair(total)
        first_ref[half, :LANES, :] = high
        first_ref[half, LANES:, :] = low

        row = lax.broadcasted_iota(jnp.int32, (TILES * LANES, LANES), 0)
        col = lax.broadcasted_iota(jnp.int32, (TILES * LANES, LANES), 1)
        sample = half * 32 + (row // LANES) * UB + row % UB
        taps = jnp.concatenate([up_ref[...]] * TILES, axis=0)
        total = jnp.zeros((TILES * LANES, LANES), jnp.float32)
        for k in range(5):
            total = total + jnp.where(col == ((2 * sample + k - 2) & (LANES - 1)), taps[:, k : k + 1], 0.0)
        high, low = split_pair(total)
        both = jnp.concatenate([high, low], axis=1)
        last_ref[half] = jnp.concatenate([both, both], axis=0)

    row = lax.broadcasted_iota(jnp.int32, (LANES, LANES), 0)
    col = lax.broadcasted_iota(jnp.int32, (LANES, LANES), 1)
    high, low = split_pair(jnp.where(row % UB == col % UB, mix_ref[...], 0.0))
    mixing_ref[:LANES, :LANES] = high
    mixing_ref[LANES:, :LANES] = high
    mixing_ref[:LANES, LANES:] = low
    mixing_ref[LANES:, LANES:] = low


def prepare(time_taps, time_bias, shot_taps, mix_weight, mix_bias, up_taps):
    lanes = jnp.concatenate(
        [time_taps.T, time_bias[None], shot_taps.T, mix_bias[None], jnp.zeros((4, time_bias.shape[0]), jnp.float32)]
    )
    lanes = jnp.repeat(lanes, UB, axis=1)
    mix = jnp.repeat(jnp.repeat(mix_weight.T, UB, axis=0), UB, axis=1)
    up = jnp.repeat(up_taps, UB, axis=0)
    mats = pl.pallas_call(
        prepare_kernel,
        out_shape=(
            jax.ShapeDtypeStruct((HALVES, 2 * LANES, TILES * LANES), jnp.bfloat16),
            jax.ShapeDtypeStruct((2 * LANES, 2 * LANES), jnp.bfloat16),
            jax.ShapeDtypeStruct((HALVES, 2 * TILES * LANES, 2 * LANES), jnp.bfloat16),
        ),
        compiler_params=pltpu.CompilerParams(vmem_limit_bytes=8 << 20),
        cost_estimate=pl.CostEstimate(flops=4_000_000, bytes_accessed=2_000_000, transcendentals=0),
    )(lanes, mix, up)
    return (lanes,) + mats


def deblend_kernel(
    shots, rcv, padded, stride, blocks,
    taken_ref, lane_ref, first_ref, mixing_ref, last_ref, out_ref,
    record, current, strided, correction, denoised, partner_ref, delay_ref,
):
    rows = shots * padded
    time_len = blocks * LANES
    base = rcv // 8 * 8
    marked = lax.broadcasted_iota(jnp.int32, (8, LANES), 0) == rcv - base
    place = lax.broadcasted_iota(jnp.int32, (8, LANES), 1)
    for shot in range(shots):
        order = taken_ref[shot * stride + base : shot * stride + base + 8, :LANES].astype(jnp.float32)
        partner_ref[shot] = jnp.sum(jnp.where(marked & (place == 0), order, 0.0)).astype(jnp.int32)
        delay_ref[shot] = jnp.sum(jnp.where(marked & (place == 1), order, 0.0)).astype(jnp.int32)
        piece = taken_ref[shot * stride : shot * stride + padded, :]
        record[shot * padded : (shot + 1) * padded, :] = piece
        current[shot * padded : (shot + 1) * padded, LANES : LANES + time_len] = piece
    zero_block = jnp.zeros((rows, LANES), jnp.bfloat16)
    current[:, :LANES] = zero_block
    current[:, (blocks + 1) * LANES :] = zero_block
    for half in range(HALVES):
        correction[half, :, :LANES] = jnp.zeros((rows, LANES), jnp.float32)
        correction[half, :, (blocks + 1) * LANES :] = jnp.zeros((rows, LANES), jnp.float32)
    lane = lax.broadcasted_iota(jnp.int32, (rows, LANES), 1)

    def one_block(block, carry):
        at = pl.multiple_of(block * LANES, LANES)
        middle = pl.multiple_of(at + LANES, LANES)
        before = current[:, pl.ds(at, LANES)]
        here = current[:, pl.ds(middle, LANES)]
        after = current[:, pl.ds(pl.multiple_of(at + 2 * LANES, LANES), LANES)]
        one = jnp.ones_like(here)
        windows = (
            jnp.where(lane >= LANES - 2, before, jnp.where(lane == ONES_LANE[0], one, here)),
            jnp.where(lane == 0, after, jnp.where(lane == ONES_LANE[1], one, here)),
        )

        def first_layer(half):
            window = jnp.concatenate([windows[half]] * 2, axis=1)
            total = jnp.dot(window, first_ref[half], preferred_element_type=jnp.float32)
            strided[:, half * TILES * LANES : (half + 1) * TILES * LANES] = jnp.maximum(total, 0.0)

        def one_tile(half, tile):
            span = slice((half * TILES + tile) * LANES, (half * TILES + tile + 1) * LANES)
            across = []
            for shot in range(shots):
                total = None
                for k in range(5):
                    source = shot + k - 2
                    if 0 <= source < shots:
                        term = strided[source * padded : (source + 1) * padded, span] * lane_ref[6 + k : 7 + k, :]
                        total = term if total is None else total + term
                across.append(total)
            high, low = split_pair(jnp.concatenate(across, axis=0))
            both = jnp.dot(jnp.concatenate([high, low], axis=1), mixing_ref[...], preferred_element_type=jnp.float32)
            return split_pair(jnp.maximum(both[:, :LANES] + both[:, LANES:] + lane_ref[11:12, :], 0.0))

        def last_layer(half, pairs):
            mixed = jnp.concatenate([pair[0] for pair in pairs] + [pair[1] for pair in pairs], axis=1)
            both = jnp.dot(mixed, last_ref[half], preferred_element_type=jnp.float32)
            correction[half, :, pl.ds(middle, LANES)] = both[:, :LANES] + both[:, LANES:]

        first_layer(0)
        pairs = [one_tile(0, 0)]
        first_layer(1)
        pairs = pairs + [one_tile(0, tile) for tile in range(1, TILES)]
        later = [one_tile(1, 0)]
        last_layer(0, pairs)
        later = later + [one_tile(1, tile) for tile in range(1, TILES)]
        last_layer(1, later)
        return carry

    def one_iteration(iteration, carry):
        lax.fori_loop(0, blocks, one_block, 0)
        for block in range(blocks):
            at = (block + 1) * LANES
            low_half = jnp.where(lane < 96, correction[0, :, at : at + LANES], correction[0, :, at + LANES : at + 2 * LANES])
            high_half = jnp.where(lane >= 32, correction[1, :, at : at + LANES], correction[1, :, at - LANES : at])
            value = current[:, at : at + LANES].astype(jnp.float32) - (low_half + high_half)
            denoised[:, at - LANES : at] = value.astype(jnp.bfloat16)
        column = lax.broadcasted_iota(jnp.int32, (padded, time_len), 1)

        def one_shot(shot, carry):
            delay = delay_ref[shot]
            here = pl.ds(pl.multiple_of(shot * padded, padded), padded)
            there = pl.ds(pl.multiple_of(partner_ref[shot] * padded, padded), padded)
            shifted = pltpu.roll(denoised[there, :].astype(jnp.float32), delay, 1)
            delayed = jnp.where(column >= delay, shifted, 0.0)
            value = denoised[here, :].astype(jnp.float32)
            original = record[here, :].astype(jnp.float32)
            current[here, LANES : LANES + time_len] = (value + 0.5 * (original - value - delayed)).astype(jnp.bfloat16)
            return carry

        lax.fori_loop(0, shots, one_shot, 0)
        return carry

    lax.fori_loop(0, ITERS, one_iteration, 0)
    out_ref[...] = current[:, LANES : LANES + time_len]


def deblend(taken, lanes, first, mixing, last, shots, rcv):
    total, time_len = taken.shape
    blocks = time_len // LANES
    padded = -(-rcv // 16) * 16
    rows = shots * padded
    wide = HALVES * TILES * LANES
    vmem = pl.BlockSpec(memory_space=pltpu.VMEM)

    def kernel(*refs):
        deblend_kernel(shots, rcv, padded, total // shots, blocks, *refs)

    return pl.pallas_call(
        kernel,
        out_shape=jax.ShapeDtypeStruct((rows, time_len), jnp.bfloat16),
        in_specs=[vmem] * 5,
        out_specs=vmem,
        scratch_shapes=[
            pltpu.VMEM((rows, time_len), jnp.bfloat16),
            pltpu.VMEM((rows, (blocks + 2) * LANES), jnp.bfloat16),
            pltpu.VMEM((rows, wide), jnp.float32),
            pltpu.VMEM((HALVES, rows, (blocks + 2) * LANES), jnp.float32),
            pltpu.VMEM((rows, time_len), jnp.bfloat16),
            pltpu.SMEM((shots,), jnp.int32),
            pltpu.SMEM((shots,), jnp.int32),
        ],
        compiler_params=pltpu.CompilerParams(vmem_limit_bytes=(8 << 20) + rows * 24576),
        cost_estimate=pl.CostEstimate(
            flops=ITERS * rows * time_len * 8 * 2 * 256 * 5, bytes_accessed=4 * rows * time_len, transcendentals=0
        ),
    )(taken, lanes, first, mixing, last)


def body(blended, partners, delays, time_taps, time_bias, shot_taps, mix_weight, mix_bias, up_taps):
    shot_count, rcv_total, time_len = blended.shape
    peers = lax.axis_size("shot")
    shots = shot_count * peers
    rcv = rcv_total // peers
    padded = -(-rcv // 16) * 16
    stride = padded + 8 if rcv == padded else padded
    mats = prepare(time_taps, time_bias, shot_taps, mix_weight, mix_bias, up_taps)
    pieces = jnp.moveaxis(blended.reshape(shot_count, peers, rcv, time_len), 1, 0)
    orders = jnp.stack([partners, delays], axis=1).astype(blended.dtype)
    orders = jnp.pad(orders[:, None, :], ((0, 0), (0, stride - rcv - 1), (0, time_len - 2)))
    orders = jnp.broadcast_to(orders[None], (peers,) + orders.shape)
    taken = lax.all_to_all(
        jnp.concatenate([pieces, orders], axis=2), "shot", split_axis=0, concat_axis=0, tiled=True
    ).reshape(shots * stride, time_len)
    done = deblend(taken, *mats, shots, rcv).reshape(shots, padded, time_len)[:, :rcv]
    pieces = done.reshape(peers, shot_count, rcv, time_len)
    back = lax.all_to_all(pieces, "shot", split_axis=0, concat_axis=0, tiled=True)
    return jnp.moveaxis(back, 0, 1).reshape(shot_count, rcv_total, time_len)


def solution(mesh):
    placed = (
        P(("groups", "shot"), None, None),
        P(("groups", "shot")),
        P(("groups", "shot")),
        P(),
        P(),
        P(),
        P(),
        P(),
        P(),
    )
    return jax.shard_map(
        body,
        mesh=mesh,
        in_specs=placed,
        out_specs=P(("groups", "shot"), None, None),
        check_vma=False,
    )
```

time: 111 us -> 88.2 us (0.79)
  blocking collectives: 51.8 us -> 26.6 us
  waiting for transfers between devices: 0.01 us -> 18.7 us
  Pallas kernels: 41.6 us -> 30 us
  local copies, waits for them, and re-layouts: 8.37 us -> 1.51 us
  other arithmetic: 0.07 us -> 2.22 us
    all_gather x1 -> x0, blocking collectives: 26.7 us -> none  [body(): lax.all_gather(jnp.stack([partners, delays]), 'shot', axis=1, tiled=True)]
    all_to_all x1, waiting for transfers between devices: 0.01 us -> 18.7 us  [body(): lax.all_to_all(jnp.concatenate([pieces, orders], axis=2), 'shot', split_a...]
    pallas_call x1, Pallas kernels: 38.5 us -> 28.5 us  [deblend(): pl.pallas_call(kernel, out_shape=jax.ShapeDtypeStruct((rows, time_len), j...]
    unnamed x22 -> x14, local copies, waits for them, and re-layouts: 5.92 us -> 0.99 us
    concatenate x0 -> x1, other arithmetic: none -> 2.15 us  [body(): jnp.concatenate([pieces, orders], axis=2)]
    pallas_call x1, Pallas kernels: 3.08 us -> 1.47 us  [prepare(): pl.pallas_call(prepare_kernel, out_shape=(jax.ShapeDtypeStruct((HALVES, 2...]
    all_to_all x1, blocking collectives: 25.1 us -> 26.6 us  [body(): lax.all_to_all(pieces, 'shot', split_axis=0, concat_axis=0, tiled=True)]
  transfers between devices with their start and end apart: 1 -> 1, of which waited for: 0 -> 1; matrix products, arithmetic and copies ran while one was open for 2% -> 1% of each run, Pallas kernels for 3% -> 2%
where the time goes in v2:
time: 88.2 us; the launch traced here: 87.9 us
  Pallas kernels  30 us (34%)
  blocking collectives  26.6 us (30%)
  waiting for transfers between devices  18.7 us (21%)
  starting transfers between devices  7.49 us (8%)
  other arithmetic  2.22 us (3%)
  local copies, waits for them, and re-layouts  1.51 us (2%)
  between operations  1.4 us (2%)
    pallas_call x1, Pallas kernels, deblend(): pl.pallas_call(kernel, out_shape=jax.ShapeDtypeStruct((rows, time_len), j...  28.5 us
    all_to_all x1, blocking collectives, body(): lax.all_to_all(pieces, 'shot', split_axis=0, concat_axis=0, tiled=True)  26.6 us
    all_to_all x1, waiting for transfers between devices, body(): lax.all_to_all(jnp.concatenate([pieces, orders], axis=2), 'shot', split_a...  18.7 us
    all_to_all x1, starting transfers between devices, body(): lax.all_to_all(jnp.concatenate([pieces, orders], axis=2), 'shot', split_a...  7.49 us
    concatenate x1, other arithmetic, body(): jnp.concatenate([pieces, orders], axis=2)  2.15 us
  transfers between devices with their start and end apart: 1, of which 1 were waited for; matrix products, arithmetic and copies ran while one was open for 1% of the time, Pallas kernels for 2%

profile of v2, /device:TPU:1, one launch (start us, length us, event | category | flops | bytes accessed | tf_op | source)
XLA Modules:
  0.0 87.9 jit_solution(980734673142168582)
XLA Ops:
  1.3 0.1 fusion.6
  1.4 2.1 %pad_maximum_fusion = bf16[16,1,56,512]{3,2,1,0:T(8,128)(2,1)} fusion(bf16[16,1,8,512]{3,2,1,0:T(8,128)(2,1)S(1)} %broadcast_in_dim.31, bf16[16,1,48,512]{3,2,1,0:T(8,128)(2,1)} %bitcast.26), kind=kLoop, calls=%fused_computation | loop fusion | flops 1835008 | bytes 1835008 | tf_op jit(solution)/shard_map/concatenate | solution.py:220
  3.5 0.0 copy-start.1
  3.5 0.0 copy-start.2
  3.6 0.0 copy-start.4
  3.6 0.0 copy-start.5
  3.6 0.0 copy-start
  3.6 0.0 copy-start.3
  3.6 7.5 %all-to-all-start = ((bf16[16,1,56,512]{3,2,1,0:T(8,128)(2,1)}), bf16[16,1,56,512]{3,2,1,0:T(8,128)(2,1)S(1)}, u32[]{:S(2)}, u32[]{:S(2)}) async-start(bf16[16,1,56,512]{3,2,1,0:T(8,128)(2,1)} %pad_maximum_fusion), calls=%async_computation | async-start | bytes 1835008 | tf_op jit(solution)/shard_map/all_to_all | solution.py:219
  11.1 0.0 copy-done.1
  11.1 0.0 copy-done.2
  11.1 0.0 copy-done.4
  11.1 0.0 copy-done.5
  11.1 0.1 concatenate.17
  11.2 0.1 copy.24
  11.3 0.0 copy-done
  11.3 0.1 copy.25
  11.4 0.0 copy-done.3
  11.4 0.1 copy.27
  11.5 0.1 copy.26
  11.5 0.1 copy.29.mix_ref
  11.7 0.1 copy.30.lane_ref.refs_1_
  11.7 1.5 %shard_map.91 = (bf16[2,256,512]{2,1,0:T(8,128)(2,1)S(1)}, bf16[256,256]{1,0:T(8,128)(2,1)S(1)}, bf16[2,1024,256]{2,1,0:T(8,128)(2,1)S(1)}) custom-call(f32[16,128]{1,0:T(8,128)S(1)} %copy.30.lane_ref.refs_1_, f32[128,128]{1,0:T(8,128)S(1)} %copy.29.mix_ref, f32[128,5]{1,0:T(8,128)S(1)} %broadcast_bitcast_fusion.up_ref), custom_call_target="tpu_custom_call" | custom-call | flops 4000000 | bytes 2000000 | tf_op jit(solution)/shard_map/pallas_call | solution.py:62
  13.2 18.7 %all-to-all-done = bf16[16,1,56,512]{3,2,1,0:T(8,128)(2,1)S(1)} async-done(((bf16[16,1,56,512]{3,2,1,0:T(8,128)(2,1)}), bf16[16,1,56,512]{3,2,1,0:T(8,128)(2,1)S(1)}, u32[]{:S(2)}, u32[]{:S(2)}) %all-to-all-start) | async-done | bytes 917536 | tf_op jit(solution)/shard_map/all_to_all | solution.py:219
  31.9 28.5 %shard_map.92 = bf16[768,512]{1,0:T(8,128)(2,1)S(1)} custom-call(bf16[896,512]{1,0:T(8,128)(2,1)S(1)} %bitcast.23, f32[16,128]{1,0:T(8,128)S(1)} %copy.30.lane_ref.refs_1_, bf16[2,256,512]{2,1,0:T(8,128)(2,1)S(1)} %get-tuple-element.8.refs_2_, bf16[256,256]{1,0:T(8,128)(2,1)S(1)} %get-tuple-element.9.refs_3_, bf16[2,1024,256]{2,1,0:T(8,128)(2,1)S(1)} %get-tuple-element.10.refs_4_), custom_call_target="tpu_custom_call" | custom-call | flops 16106127360 | bytes 1572864 | tf_op jit(solution)/shard_map/pallas_call | solution.py:186
  60.4 26.6 %all_to_all.10 = bf16[16,1,48,512]{3,2,1,0:T(8,128)(2,1)S(1)} all-to-all(bf16[16,1,48,512]{3,2,1,0:T(8,128)(2,1)S(1)} %bitcast.24), channel_id=1, replica_groups=mesh['groups'=2,'shot'=16] {'shot'}, dimensions={0} | all-to-all | bytes 1572864 | tf_op jit(solution)/shard_map/all_to_all | solution.py:224
  87.0 0.9 %copy.35 = bf16[1,768,512]{2,1,0:T(8,128)(2,1)} copy(bf16[1,768,512]{2,1,0:T(8,128)(2,1)S(1)} %bitcast.25) | data formatting | bytes 1572864
  (6 shorter events, 0.0 us)
Async XLA Ops:
  3.5 7.5 %copy-start.1 = (f32[16,5]{0,1:T(8,128)S(1)}, f32[16,5]{0,1:T(8,128)}, u32[]{:S(2)}) copy-start(f32[16,5]{0,1:T(8,128)} %param.12) | copy-start | bytes 964
  3.5 7.5 %copy-start.2 = (f32[16,5]{0,1:T(8,128)S(1)}, f32[16,5]{0,1:T(8,128)}, u32[]{:S(2)}) copy-start(f32[16,5]{0,1:T(8,128)} %param.14) | copy-start | bytes 964
  3.6 7.6 %copy-start.4 = (f32[16]{0:T(128)S(1)}, f32[16]{0:T(128)}, u32[]{:S(2)}) copy-start(f32[16]{0:T(128)} %param.13) | copy-start | bytes 196
  3.6 7.6 %copy-start.5 = (f32[16]{0:T(128)S(1)}, f32[16]{0:T(128)}, u32[]{:S(2)}) copy-start(f32[16]{0:T(128)} %param.16) | copy-start | bytes 196
  3.6 7.8 %copy-start = (f32[16,16]{1,0:T(8,128)S(1)}, f32[16,16]{1,0:T(8,128)}, u32[]{:S(2)}) copy-start(f32[16,16]{1,0:T(8,128)} %param.15) | copy-start | bytes 3076
  3.6 7.8 %copy-start.3 = (f32[16,5]{0,1:T(8,128)S(1)}, f32[16,5]{0,1:T(8,128)}, u32[]{:S(2)}) copy-start(f32[16,5]{0,1:T(8,128)} %param.17) | copy-start | bytes 964
  3.6 28.3 %all-to-all-start = ((bf16[16,1,56,512]{3,2,1,0:T(8,128)(2,1)}), bf16[16,1,56,512]{3,2,1,0:T(8,128)(2,1)S(1)}, u32[]{:S(2)}, u32[]{:S(2)}) async-start(bf16[16,1,56,512]{3,2,1,0:T(8,128)(2,1)} %pad_maximum_fusion), calls=%async_computation | async-start | bytes 1835008 | tf_op jit(solution)/shard_map/all_to_all | solution.py:219

commit v3 on v2

--- a/solution.py
+++ b/solution.py
@@ -7,6 +7,7 @@
 
 ITERS = 2
 LANES = 128
+SUBLANES = 8
 UB = 8
 HALVES = 2
 TILES = 4
@@ -73,22 +74,25 @@
 
 
 def deblend_kernel(
-    shots, rcv, padded, stride, blocks,
+    shots, padded, blocks,
     taken_ref, lane_ref, first_ref, mixing_ref, last_ref, out_ref,
     record, current, strided, correction, denoised, partner_ref, delay_ref,
 ):
     rows = shots * padded
     time_len = blocks * LANES
-    base = rcv // 8 * 8
-    marked = lax.broadcasted_iota(jnp.int32, (8, LANES), 0) == rcv - base
-    place = lax.broadcasted_iota(jnp.int32, (8, LANES), 1)
+    tiles = padded // SUBLANES * blocks
+    lane = lax.broadcasted_iota(jnp.int32, (SUBLANES, LANES), 1)
+    first_row = lax.broadcasted_iota(jnp.int32, (SUBLANES, LANES), 0) == 0
     for shot in range(shots):
-        order = taken_ref[shot * stride + base : shot * stride + base + 8, :LANES].astype(jnp.float32)
-        partner_ref[shot] = jnp.sum(jnp.where(marked & (place == 0), order, 0.0)).astype(jnp.int32)
-        delay_ref[shot] = jnp.sum(jnp.where(marked & (place == 1), order, 0.0)).astype(jnp.int32)
-        piece = taken_ref[shot * stride : shot * stride + padded, :]
-        record[shot * padded : (shot + 1) * padded, :] = piece
-        current[shot * padded : (shot + 1) * padded, LANES : LANES + time_len] = piece
+        order = taken_ref[shot, tiles].astype(jnp.float32)
+        partner_ref[shot] = jnp.sum(jnp.where(first_row & (lane == 0), order, 0.0)).astype(jnp.int32)
+        delay_ref[shot] = jnp.sum(jnp.where(first_row & (lane == 1), order, 0.0)).astype(jnp.int32)
+        for block in range(blocks):
+            pieces = [taken_ref[shot, group * blocks + block] for group in range(padded // SUBLANES)]
+            piece = jnp.concatenate(pieces, axis=0)
+            place = slice(shot * padded, (shot + 1) * padded)
+            record[place, block * LANES : (block + 1) * LANES] = piece
+            current[place, (block + 1) * LANES : (block + 2) * LANES] = piece
     zero_block = jnp.zeros((rows, LANES), jnp.bfloat16)
     current[:, :LANES] = zero_block
     current[:, (blocks + 1) * LANES :] = zero_block
@@ -97,12 +101,12 @@
         correction[half, :, (blocks + 1) * LANES :] = jnp.zeros((rows, LANES), jnp.float32)
     lane = lax.broadcasted_iota(jnp.int32, (rows, LANES), 1)
 
-    def one_block(block, carry):
-        at = pl.multiple_of(block * LANES, LANES)
-        middle = pl.multiple_of(at + LANES, LANES)
-        before = current[:, pl.ds(at, LANES)]
-        here = current[:, pl.ds(middle, LANES)]
-        after = current[:, pl.ds(pl.multiple_of(at + 2 * LANES, LANES), LANES)]
+    def one_block(block):
+        at = block * LANES
+        middle = at + LANES
+        before = current[:, at : at + LANES]
+        here = current[:, middle : middle + LANES]
+        after = current[:, middle + LANES : middle + 2 * LANES]
         one = jnp.ones_like(here)
         windows = (
             jnp.where(lane >= LANES - 2, before, jnp.where(lane == ONES_LANE[0], one, here)),
@@ -132,7 +136,7 @@
         def last_layer(half, pairs):
             mixed = jnp.concatenate([pair[0] for pair in pairs] + [pair[1] for pair in pairs], axis=1)
             both = jnp.dot(mixed, last_ref[half], preferred_element_type=jnp.float32)
-            correction[half, :, pl.ds(middle, LANES)] = both[:, :LANES] + both[:, LANES:]
+            correction[half, :, middle : middle + LANES] = both[:, :LANES] + both[:, LANES:]
 
         first_layer(0)
         pairs = [one_tile(0, 0)]
@@ -142,10 +146,10 @@
         last_layer(0, pairs)
         later = later + [one_tile(1, tile) for tile in range(1, TILES)]
         last_layer(1, later)
-        return carry
 
     def one_iteration(iteration, carry):
-        lax.fori_loop(0, blocks, one_block, 0)
+        for block in range(blocks):
+            one_block(block)
         for block in range(blocks):
             at = (block + 1) * LANES
             low_half = jnp.where(lane < 96, correction[0, :, at : at + LANES], correction[0, :, at + LANES : at + 2 * LANES])
@@ -165,23 +169,21 @@
             current[here, LANES : LANES + time_len] = (value + 0.5 * (original - value - delayed)).astype(jnp.bfloat16)
             return carry
 
-        lax.fori_loop(0, shots, one_shot, 0)
+        lax.fori_loop(0, shots, one_shot, 0, unroll=4)
         return carry
 
     lax.fori_loop(0, ITERS, one_iteration, 0)
     out_ref[...] = current[:, LANES : LANES + time_len]
 
 
-def deblend(taken, lanes, first, mixing, last, shots, rcv):
-    total, time_len = taken.shape
+def deblend(taken, lanes, first, mixing, last, shots, padded, time_len):
     blocks = time_len // LANES
-    padded = -(-rcv // 16) * 16
     rows = shots * padded
     wide = HALVES * TILES * LANES
     vmem = pl.BlockSpec(memory_space=pltpu.VMEM)
 
     def kernel(*refs):
-        deblend_kernel(shots, rcv, padded, total // shots, blocks, *refs)
+        deblend_kernel(shots, padded, blocks, *refs)
 
     return pl.pallas_call(
         kernel,
@@ -209,17 +211,22 @@
     peers = lax.axis_size("shot")
     shots = shot_count * peers
     rcv = rcv_total // peers
-    padded = -(-rcv // 16) * 16
-    stride = padded + 8 if rcv == padded else padded
+    padded = -(-rcv // SUBLANES) * SUBLANES
+    blocks = time_len // LANES
     mats = prepare(time_taps, time_bias, shot_taps, mix_weight, mix_bias, up_taps)
     pieces = jnp.moveaxis(blended.reshape(shot_count, peers, rcv, time_len), 1, 0)
+    pieces = jnp.pad(pieces, ((0, 0), (0, 0), (0, padded - rcv), (0, 0)))
+    pieces = jnp.swapaxes(
+        pieces.reshape(peers, shot_count, padded // SUBLANES, SUBLANES, blocks, LANES), 3, 4
+    ).reshape(peers, shot_count, padded // SUBLANES * blocks, SUBLANES, LANES)
     orders = jnp.stack([partners, delays], axis=1).astype(blended.dtype)
-    orders = jnp.pad(orders[:, None, :], ((0, 0), (0, stride - rcv - 1), (0, time_len - 2)))
+    orders = jnp.pad(orders[:, None, None, :], ((0, 0), (0, 0), (0, SUBLANES - 1), (0, LANES - 2)))
     orders = jnp.broadcast_to(orders[None], (peers,) + orders.shape)
     taken = lax.all_to_all(
         jnp.concatenate([pieces, orders], axis=2), "shot", split_axis=0, concat_axis=0, tiled=True
-    ).reshape(shots * stride, time_len)
-    done = deblend(taken, *mats, shots, rcv).reshape(shots, padded, time_len)[:, :rcv]
+    )
+    taken = taken.reshape((shots,) + taken.shape[2:])
+    done = deblend(taken, *mats, shots, padded, time_len).reshape(shots, padded, time_len)[:, :rcv]
     pieces = done.reshape(peers, shot_count, rcv, time_len)
     back = lax.all_to_all(pieces, "shot", split_axis=0, concat_axis=0, tiled=True)
     return jnp.moveaxis(back, 0, 1).reshape(shot_count, rcv_total, time_len)

time: 88.2 us -> 82.2 us (0.932)
  Pallas kernels: 30 us -> 26.1 us
  waiting for transfers between devices: 18.7 us -> 15.1 us
  local copies, waits for them, and re-layouts: 1.51 us -> 3.35 us
    pallas_call x1, Pallas kernels: 28.5 us -> 24.6 us  [deblend(): pl.pallas_call(kernel, out_shape=jax.ShapeDtypeStruct((rows, time_len), j...]
    all_to_all x1, waiting for transfers between devices: 18.7 us -> 15.1 us  [body(): lax.all_to_all(jnp.concatenate([pieces, orders], axis=2), 'shot', split_a...]
    unnamed x14, local copies, waits for them, and re-layouts: 0.99 us -> 2.87 us
where the time goes in v3:
time: 82.2 us; the launch traced here: 81.8 us
  blocking collectives  26.2 us (32%)
  Pallas kernels  26.1 us (32%)
  waiting for transfers between devices  15.1 us (18%)
  starting transfers between devices  7.48 us (9%)
  local copies, waits for them, and re-layouts  3.35 us (4%)
  other arithmetic  2.17 us (3%)
  between operations  1.39 us (2%)
    all_to_all x1, blocking collectives, body(): lax.all_to_all(pieces, 'shot', split_axis=0, concat_axis=0, tiled=True)  26.2 us
    pallas_call x1, Pallas kernels, deblend(): pl.pallas_call(kernel, out_shape=jax.ShapeDtypeStruct((rows, time_len), j...  24.6 us
    all_to_all x1, waiting for transfers between devices, body(): lax.all_to_all(jnp.concatenate([pieces, orders], axis=2), 'shot', split_a...  15.1 us
    all_to_all x1, starting transfers between devices, body(): lax.all_to_all(jnp.concatenate([pieces, orders], axis=2), 'shot', split_a...  7.48 us
    unnamed x14, local copies, waits for them, and re-layouts  2.87 us
    concatenate x1, other arithmetic, body(): jnp.concatenate([pieces, orders], axis=2)  2.09 us
  transfers between devices with their start and end apart: 1, of which 1 were waited for; matrix products, arithmetic and copies ran while one was open for 1% of the time, Pallas kernels for 2%

profile of v3, /device:TPU:1, one launch (start us, length us, event | category | flops | bytes accessed | tf_op | source)
XLA Modules:
  0.0 81.8 jit_solution(11802305182998897534)
XLA Ops:
  1.3 0.1 fusion.6
  1.4 2.1 %pad_maximum_fusion = bf16[16,1,25,8,128]{4,3,2,1,0:T(8,128)(2,1)} fusion(bf16[16,1,1,8,128]{4,3,2,1,0:T(8,128)(2,1)S(1)} %broadcast_in_dim.31, bf16[16,1,24,8,128]{4,3,2,1,0:T(8,128)(2,1)} %bitcast.30), kind=kLoop, calls=%fused_computation | loop fusion | flops 409600 | bytes 1638400 | tf_op jit(solution)/shard_map/concatenate | solution.py:226
  3.5 0.0 copy-start.4
  3.5 0.0 copy-start.5
  3.5 7.5 %all-to-all-start = ((bf16[16,1,25,8,128]{4,3,2,1,0:T(8,128)(2,1)}), bf16[16,1,25,8,128]{4,3,2,1,0:T(8,128)(2,1)S(1)}, u32[]{:S(2)}, u32[]{:S(2)}) async-start(bf16[16,1,25,8,128]{4,3,2,1,0:T(8,128)(2,1)} %pad_maximum_fusion), calls=%async_computation | async-start | bytes 1638400 | tf_op jit(solution)/shard_map/all_to_all | solution.py:225
  11.0 0.0 copy-start.1
  11.0 0.0 copy-start.2
  11.0 0.0 copy-done.4
  11.0 0.0 copy-done.5
  11.0 0.6 copy-done.1
  11.7 0.0 copy-done.2
  11.7 0.1 concatenate.17
  11.8 0.0 copy-start
  11.8 0.1 copy.24
  11.9 0.6 copy-done
  12.5 0.0 copy-start.3
  12.5 0.1 copy.25
  12.5 0.6 copy-done.3
  13.2 0.1 copy.27
  13.3 0.1 copy.26
  13.3 0.1 copy.29.mix_ref
  13.4 0.1 copy.30.lane_ref.refs_1_
  13.5 1.5 %shard_map.91 = (bf16[2,256,512]{2,1,0:T(8,128)(2,1)S(1)}, bf16[256,256]{1,0:T(8,128)(2,1)S(1)}, bf16[2,1024,256]{2,1,0:T(8,128)(2,1)S(1)}) custom-call(f32[16,128]{1,0:T(8,128)S(1)} %copy.30.lane_ref.refs_1_, f32[128,128]{1,0:T(8,128)S(1)} %copy.29.mix_ref, f32[128,5]{1,0:T(8,128)S(1)} %broadcast_bitcast_fusion.up_ref), custom_call_target="tpu_custom_call" | custom-call | flops 4000000 | bytes 2000000 | tf_op jit(solution)/shard_map/pallas_call | solution.py:63
  15.0 15.1 %all-to-all-done = bf16[16,1,25,8,128]{4,3,2,1,0:T(8,128)(2,1)S(1)} async-done(((bf16[16,1,25,8,128]{4,3,2,1,0:T(8,128)(2,1)}), bf16[16,1,25,8,128]{4,3,2,1,0:T(8,128)(2,1)S(1)}, u32[]{:S(2)}, u32[]{:S(2)}) %all-to-all-start) | async-done | bytes 819232 | tf_op jit(solution)/shard_map/all_to_all | solution.py:225
  30.1 24.6 %shard_map.92 = bf16[768,512]{1,0:T(8,128)(2,1)S(1)} custom-call(bf16[16,25,8,128]{3,2,1,0:T(8,128)(2,1)S(1)} %bitcast.27, f32[16,128]{1,0:T(8,128)S(1)} %copy.30.lane_ref.refs_1_, bf16[2,256,512]{2,1,0:T(8,128)(2,1)S(1)} %get-tuple-element.8.refs_2_, bf16[256,256]{1,0:T(8,128)(2,1)S(1)} %get-tuple-element.9.refs_3_, ...), custom_call_target="tpu_custom_call" | custom-call | flops 16106127360 | bytes 1572864 | tf_op jit(solution)/shard_map/pallas_call | solution.py:188
  54.7 26.2 %all_to_all.10 = bf16[16,1,48,512]{3,2,1,0:T(8,128)(2,1)S(1)} all-to-all(bf16[16,1,48,512]{3,2,1,0:T(8,128)(2,1)S(1)} %bitcast.28), channel_id=1, replica_groups=mesh['groups'=2,'shot'=16] {'shot'}, dimensions={0} | all-to-all | bytes 1572864 | tf_op jit(solution)/shard_map/all_to_all | solution.py:231
  80.9 0.9 %copy.35 = bf16[1,768,512]{2,1,0:T(8,128)(2,1)} copy(bf16[1,768,512]{2,1,0:T(8,128)(2,1)S(1)} %bitcast.29) | data formatting | bytes 1572864
  (6 shorter events, 0.0 us)
Async XLA Ops:
  3.5 7.5 %copy-start.4 = (f32[16]{0:T(128)S(1)}, f32[16]{0:T(128)}, u32[]{:S(2)}) copy-start(f32[16]{0:T(128)} %param.13) | copy-start | bytes 196
  3.5 7.5 %copy-start.5 = (f32[16]{0:T(128)S(1)}, f32[16]{0:T(128)}, u32[]{:S(2)}) copy-start(f32[16]{0:T(128)} %param.16) | copy-start | bytes 196
  3.5 26.6 %all-to-all-start = ((bf16[16,1,25,8,128]{4,3,2,1,0:T(8,128)(2,1)}), bf16[16,1,25,8,128]{4,3,2,1,0:T(8,128)(2,1)S(1)}, u32[]{:S(2)}, u32[]{:S(2)}) async-start(bf16[16,1,25,8,128]{4,3,2,1,0:T(8,128)(2,1)} %pad_maximum_fusion), calls=%async_computation | async-start | bytes 1638400 | tf_op jit(solution)/shard_map/all_to_all | solution.py:225
  11.0 0.7 copy-start.1
  11.0 0.7 copy-start.2
  11.8 0.7 copy-start
  12.5 0.7 copy-start.3

commit v4 on v3

--- a/solution.py
+++ b/solution.py
@@ -9,6 +9,7 @@
 LANES = 128
 SUBLANES = 8
 UB = 8
+PARTS = 2
 HALVES = 2
 TILES = 4
 ONES_LANE = (96, 32)
@@ -53,13 +54,18 @@
     mixing_ref[LANES:, LANES:] = low
 
 
-def prepare(time_taps, time_bias, shot_taps, mix_weight, mix_bias, up_taps):
+def prepare(time_taps, time_bias, shot_taps, mix_weight, mix_bias, up_taps, time_len):
     lanes = jnp.concatenate(
         [time_taps.T, time_bias[None], shot_taps.T, mix_bias[None], jnp.zeros((4, time_bias.shape[0]), jnp.float32)]
     )
     lanes = jnp.repeat(lanes, UB, axis=1)
     mix = jnp.repeat(jnp.repeat(mix_weight.T, UB, axis=0), UB, axis=1)
     up = jnp.repeat(up_taps, UB, axis=0)
+    level = jnp.sum(up_taps * mix_bias[:, None], axis=0)
+    sample = jnp.arange(time_len)
+    reached = [(sample + 2 - k) % 2 == 0 for k in range(5)]
+    reached = [fits & (sample + 2 >= k) & (sample + 2 - k < time_len) for k, fits in enumerate(reached)]
+    level = sum(jnp.where(fits, level[k], 0.0) for k, fits in enumerate(reached))[None]
     mats = pl.pallas_call(
         prepare_kernel,
         out_shape=(
@@ -70,12 +76,12 @@
         compiler_params=pltpu.CompilerParams(vmem_limit_bytes=8 << 20),
         cost_estimate=pl.CostEstimate(flops=4_000_000, bytes_accessed=2_000_000, transcendentals=0),
     )(lanes, mix, up)
-    return (lanes,) + mats
+    return (level, lanes) + tuple(mats)
 
 
 def deblend_kernel(
     shots, padded, blocks,
-    taken_ref, lane_ref, first_ref, mixing_ref, last_ref, out_ref,
+    taken_ref, level_ref, lane_ref, first_ref, mixing_ref, last_ref, out_ref,
     record, current, strided, correction, denoised, partner_ref, delay_ref,
 ):
     rows = shots * padded
@@ -101,60 +107,87 @@
         correction[half, :, (blocks + 1) * LANES :] = jnp.zeros((rows, LANES), jnp.float32)
     lane = lax.broadcasted_iota(jnp.int32, (rows, LANES), 1)
 
-    def one_block(block):
+    def windows_of(block):
         at = block * LANES
         middle = at + LANES
         before = current[:, at : at + LANES]
         here = current[:, middle : middle + LANES]
         after = current[:, middle + LANES : middle + 2 * LANES]
         one = jnp.ones_like(here)
-        windows = (
+        return (
             jnp.where(lane >= LANES - 2, before, jnp.where(lane == ONES_LANE[0], one, here)),
             jnp.where(lane == 0, after, jnp.where(lane == ONES_LANE[1], one, here)),
         )
 
-        def first_layer(half):
-            window = jnp.concatenate([windows[half]] * 2, axis=1)
-            total = jnp.dot(window, first_ref[half], preferred_element_type=jnp.float32)
-            strided[:, half * TILES * LANES : (half + 1) * TILES * LANES] = jnp.maximum(total, 0.0)
-
-        def one_tile(half, tile):
-            span = slice((half * TILES + tile) * LANES, (half * TILES + tile + 1) * LANES)
-            across = []
-            for shot in range(shots):
-                total = None
-                for k in range(5):
-                    source = shot + k - 2
-                    if 0 <= source < shots:
-                        term = strided[source * padded : (source + 1) * padded, span] * lane_ref[6 + k : 7 + k, :]
-                        total = term if total is None else total + term
-                across.append(total)
-            high, low = split_pair(jnp.concatenate(across, axis=0))
-            both = jnp.dot(jnp.concatenate([high, low], axis=1), mixing_ref[...], preferred_element_type=jnp.float32)
-            return split_pair(jnp.maximum(both[:, :LANES] + both[:, LANES:] + lane_ref[11:12, :], 0.0))
-
-        def last_layer(half, pairs):
-            mixed = jnp.concatenate([pair[0] for pair in pairs] + [pair[1] for pair in pairs], axis=1)
-            both = jnp.dot(mixed, last_ref[half], preferred_element_type=jnp.float32)
-            correction[half, :, middle : middle + LANES] = both[:, :LANES] + both[:, LANES:]
-
-        first_layer(0)
-        pairs = [one_tile(0, 0)]
-        first_layer(1)
-        pairs = pairs + [one_tile(0, tile) for tile in range(1, TILES)]
-        later = [one_tile(1, 0)]
-        last_layer(0, pairs)
-        later = later + [one_tile(1, tile) for tile in range(1, TILES)]
-        last_layer(1, later)
+    def first_layer(block, half, pair):
+        span = slice(pair * 2 * LANES, (pair + 1) * 2 * LANES)
+        window = jnp.concatenate([windows[block][half]] * 2, axis=1)
+        total = jnp.dot(window, first_ref[half, :, span], preferred_element_type=jnp.float32)
+        start = half * TILES * LANES
+        strided[:, start + span.start : start + span.stop] = jnp.maximum(total, 0.0)
+
+    def shot_filter(half, tile):
+        span = slice((half * TILES + tile) * LANES, (half * TILES + tile + 1) * LANES)
+        across = []
+        for shot in range(shots):
+            total = None
+            for k in range(5):
+                source = shot + k - 2
+                if 0 <= source < shots:
+                    term = strided[source * padded : (source + 1) * padded, span] * lane_ref[6 + k : 7 + k, :]
+                    total = term if total is None else total + term
+            across.append(total)
+        return split_pair(jnp.concatenate(across, axis=0))
+
+    def mix(pair):
+        both = jnp.dot(jnp.concatenate(pair, axis=1), mixing_ref[...], preferred_element_type=jnp.float32)
+        return split_pair(jnp.maximum(both[:, :LANES] + both[:, LANES:], -lane_ref[11:12, :]))
+
+    def last_layer(block, half, pairs, part):
+        span = slice(part * rows // PARTS, (part + 1) * rows // PARTS)
+        mixed = [pair[0][span] for pair in pairs] + [pair[1][span] for pair in pairs]
+        both = jnp.dot(jnp.concatenate(mixed, axis=1), last_ref[half], preferred_element_type=jnp.float32)
+        correction[half, span, (block + 1) * LANES : (block + 2) * LANES] = both[:, :LANES] + both[:, LANES:]
+
+    windows = {}
 
     def one_iteration(iteration, carry):
-        for block in range(blocks):
-            one_block(block)
+        halves = [(block, half) for block in range(blocks) for half in range(HALVES)]
+        windows[0] = windows_of(0)
+        for pair in range(TILES // 2):
+            first_layer(0, 0, pair)
+        before = []
+        for number, (block, half) in enumerate(halves):
+            after = []
+            if number + 1 < len(halves):
+                following = halves[number + 1]
+                if following[0] not in windows:
+                    windows[following[0]] = windows_of(following[0])
+                after = [lambda pair=pair, at=following: first_layer(*at, pair) for pair in range(TILES // 2)]
+            beside = []
+            while before or after:
+                beside = beside + before[:1] + after[:1]
+                before, after = before[1:], after[1:]
+            pairs = []
+            for tile in range(TILES):
+                filtered = shot_filter(half, tile)
+                share = -(-len(beside) // (TILES - tile))
+                for step in beside[:share]:
+                    step()
+                beside = beside[share:]
+                pairs.append(mix(filtered))
+            before = [
+                lambda at=(block, half), pairs=pairs, part=part: last_layer(*at, pairs, part) for part in range(PARTS)
+            ]
+        for step in before:
+            step()
+        windows.clear()
         for block in range(blocks):
             at = (block + 1) * LANES
             low_half = jnp.where(lane < 96, correction[0, :, at : at + LANES], correction[0, :, at + LANES : at + 2 * LANES])
             high_half = jnp.where(lane >= 32, correction[1, :, at : at + LANES], correction[1, :, at - LANES : at])
-            value = current[:, at : at + LANES].astype(jnp.float32) - (low_half + high_half)
+            total = low_half + high_half + level_ref[:, at - LANES : at]
+            value = current[:, at : at + LANES].astype(jnp.float32) - total
             denoised[:, at - LANES : at] = value.astype(jnp.bfloat16)
         column = lax.broadcasted_iota(jnp.int32, (padded, time_len), 1)
 
@@ -176,7 +209,7 @@
     out_ref[...] = current[:, LANES : LANES + time_len]
 
 
-def deblend(taken, lanes, first, mixing, last, shots, padded, time_len):
+def deblend(taken, level, lanes, first, mixing, last, shots, padded, time_len):
     blocks = time_len // LANES
     rows = shots * padded
     wide = HALVES * TILES * LANES
@@ -188,7 +221,7 @@
     return pl.pallas_call(
         kernel,
         out_shape=jax.ShapeDtypeStruct((rows, time_len), jnp.bfloat16),
-        in_specs=[vmem] * 5,
+        in_specs=[vmem] * 6,
         out_specs=vmem,
         scratch_shapes=[
             pltpu.VMEM((rows, time_len), jnp.bfloat16),
@@ -203,7 +236,7 @@
         cost_estimate=pl.CostEstimate(
             flops=ITERS * rows * time_len * 8 * 2 * 256 * 5, bytes_accessed=4 * rows * time_len, transcendentals=0
         ),
-    )(taken, lanes, first, mixing, last)
+    )(taken, level, lanes, first, mixing, last)
 
 
 def body(blended, partners, delays, time_taps, time_bias, shot_taps, mix_weight, mix_bias, up_taps):
@@ -213,7 +246,7 @@
     rcv = rcv_total // peers
     padded = -(-rcv // SUBLANES) * SUBLANES
     blocks = time_len // LANES
-    mats = prepare(time_taps, time_bias, shot_taps, mix_weight, mix_bias, up_taps)
+    mats = prepare(time_taps, time_bias, shot_taps, mix_weight, mix_bias, up_taps, time_len)
     pieces = jnp.moveaxis(blended.reshape(shot_count, peers, rcv, time_len), 1, 0)
     pieces = jnp.pad(pieces, ((0, 0), (0, 0), (0, padded - rcv), (0, 0)))
     pieces = jnp.swapaxes(

time: 82.2 us -> 80.5 us (0.979)
  waiting for transfers between devices: 15.1 us -> 11.2 us
  other arithmetic: 2.17 us -> 5.44 us
  Pallas kernels: 26.1 us -> 24.3 us
    all_to_all x1, waiting for transfers between devices: 15.1 us -> 11.2 us  [body(): lax.all_to_all(jnp.concatenate([pieces, orders], axis=2), 'shot', split_a...]
    add x0 -> x1, other arithmetic: none -> 3.15 us  [prepare(): sum((jnp.where(fits, level[k], 0.0) for k, fits in enumerate(reached)))]
    pallas_call x1, Pallas kernels: 24.6 us -> 22.8 us  [deblend(): pl.pallas_call(kernel, out_shape=jax.ShapeDtypeStruct((rows, time_len), j...]
  transfers between devices with their start and end apart: 1 -> 1, of which waited for: 1 -> 1; matrix products, arithmetic and copies ran while one was open for 1% -> 6% of each run, Pallas kernels for 2% -> 2%
where the time goes in v4:
time: 80.5 us; the launch traced here: 80 us
  blocking collectives  26.2 us (33%)
  Pallas kernels  24.3 us (30%)
  waiting for transfers between devices  11.2 us (14%)
  starting transfers between devices  7.48 us (9%)
  other arithmetic  5.44 us (7%)
  local copies, waits for them, and re-layouts  4.01 us (5%)
  between operations  1.4 us (2%)
    all_to_all x1, blocking collectives, body(): lax.all_to_all(pieces, 'shot', split_axis=0, concat_axis=0, tiled=True)  26.2 us
    pallas_call x1, Pallas kernels, deblend(): pl.pallas_call(kernel, out_shape=jax.ShapeDtypeStruct((rows, time_len), j...  22.8 us
    all_to_all x1, waiting for transfers between devices, body(): lax.all_to_all(jnp.concatenate([pieces, orders], axis=2), 'shot', split_a...  11.2 us
    all_to_all x1, starting transfers between devices, body(): lax.all_to_all(jnp.concatenate([pieces, orders], axis=2), 'shot', split_a...  7.48 us
    add x1, other arithmetic, prepare(): sum((jnp.where(fits, level[k], 0.0) for k, fits in enumerate(reached)))  3.15 us
    unnamed x14, local copies, waits for them, and re-layouts  2.87 us
    concatenate x1, other arithmetic, body(): jnp.concatenate([pieces, orders], axis=2)  2.1 us
  transfers between devices with their start and end apart: 1, of which 1 were waited for; matrix products, arithmetic and copies ran while one was open for 6% of the time, Pallas kernels for 2%

profile of v4, /device:TPU:1, one launch (start us, length us, event | category | flops | bytes accessed | tf_op | source)
XLA Modules:
  0.0 80.0 jit_solution(9618850494333981553)
XLA Ops:
  1.3 0.1 fusion.8
  1.4 2.1 %pad_maximum_fusion = bf16[16,1,25,8,128]{4,3,2,1,0:T(8,128)(2,1)} fusion(bf16[16,1,1,8,128]{4,3,2,1,0:T(8,128)(2,1)S(1)} %broadcast_in_dim.57, bf16[16,1,24,8,128]{4,3,2,1,0:T(8,128)(2,1)} %bitcast.35), kind=kLoop, calls=%fused_computation | loop fusion | flops 409600 | bytes 1638400 | tf_op jit(solution)/shard_map/concatenate | solution.py:259
  3.5 0.0 copy-start.4
  3.5 0.0 copy-start.5
  3.5 7.5 %all-to-all-start = ((bf16[16,1,25,8,128]{4,3,2,1,0:T(8,128)(2,1)}), bf16[16,1,25,8,128]{4,3,2,1,0:T(8,128)(2,1)S(1)}, u32[]{:S(2)}, u32[]{:S(2)}) async-start(bf16[16,1,25,8,128]{4,3,2,1,0:T(8,128)(2,1)} %pad_maximum_fusion), calls=%async_computation | async-start | bytes 1638400 | tf_op jit(solution)/shard_map/all_to_all | solution.py:258
  11.0 0.0 copy-start.2
  11.0 0.0 copy-start.3
  11.0 0.0 copy-done.4
  11.0 0.0 copy-done.5
  11.0 0.6 copy-done.2
  11.7 0.0 copy-done.3
  11.7 0.1 concatenate.17
  11.8 0.0 copy-start.1
  11.8 0.1 copy.24
  11.9 0.6 copy-done.1
  12.5 0.0 copy-start
  12.5 0.1 copy.25
  12.6 0.6 copy-done
  13.2 0.1 copy.27
  13.3 0.1 copy.26
  13.3 0.1 copy.29.mix_ref
  13.4 0.1 copy.30.lane_ref.refs_2_
  13.5 1.5 %shard_map.91 = (bf16[2,256,512]{2,1,0:T(8,128)(2,1)S(1)}, bf16[256,256]{1,0:T(8,128)(2,1)S(1)}, bf16[2,1024,256]{2,1,0:T(8,128)(2,1)S(1)}) custom-call(f32[16,128]{1,0:T(8,128)S(1)} %copy.30.lane_ref.refs_2_, f32[128,128]{1,0:T(8,128)S(1)} %copy.29.mix_ref, f32[128,5]{1,0:T(8,128)S(1)} %broadcast_bitcast_fusion.up_ref), custom_call_target="tpu_custom_call" | custom-call | flops 4000000 | bytes 2000000 | tf_op jit(solution)/shard_map/pallas_call | solution.py:69
  15.0 0.1 multiply_reduce_fusion
  15.1 0.7 fusion.15
  15.8 3.2 %fusion.14.refs_1_ = f32[1,512]{1,0:T(1,128)S(1)} fusion(f32[]{:T(128)} %bitcast.11, f32[]{:T(128)} %bitcast.10, f32[]{:T(128)} %bitcast.9, f32[]{:T(128)} %bitcast.8, f32[]{:T(128)} %bitcast.7), kind=kLoop, calls=%fused_computation.41 | loop fusion | flops 45056 | bytes 2068 | tf_op jit(solution)/shard_map/add | solution.py:68
  18.9 11.2 %all-to-all-done = bf16[16,1,25,8,128]{4,3,2,1,0:T(8,128)(2,1)S(1)} async-done(((bf16[16,1,25,8,128]{4,3,2,1,0:T(8,128)(2,1)}), bf16[16,1,25,8,128]{4,3,2,1,0:T(8,128)(2,1)S(1)}, u32[]{:S(2)}, u32[]{:S(2)}) %all-to-all-start) | async-done | bytes 819232 | tf_op jit(solution)/shard_map/all_to_all | solution.py:258
  30.1 22.8 %shard_map.92 = bf16[768,512]{1,0:T(8,128)(2,1)S(1)} custom-call(bf16[16,25,8,128]{3,2,1,0:T(8,128)(2,1)S(1)} %bitcast.32, f32[1,512]{1,0:T(1,128)S(1)} %fusion.14.refs_1_, f32[16,128]{1,0:T(8,128)S(1)} %copy.30.lane_ref.refs_2_, bf16[2,256,512]{2,1,0:T(8,128)(2,1)S(1)} %get-tuple-element.8.refs_3_, bf16[256,256]{1,0:T(8,128)(2,1)S(1)} %get-tuple-element.9.refs_4_, ...), custom_call_target="tpu_custom_call" | custom-call | flops 16106127360 | bytes 1572864 | tf_op jit(solution)/shard_map/pallas_call | solution.py:221
  52.9 26.2 %all_to_all.10 = bf16[16,1,48,512]{3,2,1,0:T(8,128)(2,1)S(1)} all-to-all(bf16[16,1,48,512]{3,2,1,0:T(8,128)(2,1)S(1)} %bitcast.33), channel_id=1, replica_groups=mesh['groups'=2,'shot'=16] {'shot'}, dimensions={0} | all-to-all | bytes 1572864 | tf_op jit(solution)/shard_map/all_to_all | solution.py:264
  79.1 0.9 %copy.35 = bf16[1,768,512]{2,1,0:T(8,128)(2,1)} copy(bf16[1,768,512]{2,1,0:T(8,128)(2,1)S(1)} %bitcast.34) | data formatting | bytes 1572864
  (6 shorter events, 0.0 us)
Async XLA Ops:
  3.5 7.5 %copy-start.4 = (f32[16]{0:T(128)S(1)}, f32[16]{0:T(128)}, u32[]{:S(2)}) copy-start(f32[16]{0:T(128)} %param.16) | copy-start | bytes 196
  3.5 7.5 %copy-start.5 = (f32[16]{0:T(128)S(1)}, f32[16]{0:T(128)}, u32[]{:S(2)}) copy-start(f32[16]{0:T(128)} %param.13) | copy-start | bytes 196
  3.5 26.6 %all-to-all-start = ((bf16[16,1,25,8,128]{4,3,2,1,0:T(8,128)(2,1)}), bf16[16,1,25,8,128]{4,3,2,1,0:T(8,128)(2,1)S(1)}, u32[]{:S(2)}, u32[]{:S(2)}) async-start(bf16[16,1,25,8,128]{4,3,2,1,0:T(8,128)(2,1)} %pad_maximum_fusion), calls=%async_computation | async-start | bytes 1638400 | tf_op jit(solution)/shard_map/all_to_all | solution.py:258
  11.0 0.7 copy-start.2
  11.0 0.7 copy-start.3
  11.8 0.7 copy-start.1
  12.5 0.7 copy-start
